TPU v7x, 256 devices: a whole 4x4x8 slice. The times are simulated.
256 devices in a mesh: row: 16 (over x, y), col: 8 (over z_lo, core), layer: 2 (over z_hi).
Axes of the slice: x: 4, y: 4, z: 8 (z_hi: 2, z_lo: 4; z = z_hi * 4 + z_lo), core: 2. Of those that a mesh axis runs over, the one named last changes fastest.
Arguments:
- tasks: bfloat16 [16384, 4096], P(('row', 'col')), may hold values from -0.1875 to 0.1875
- task_owner: int32 [16384, 1], P(('row', 'col')), may hold values from 0 to 127; in each aligned block of 128 rows (0 to 127, 128 to 255, ...) at most 2 rows name the same one
- task_slot: int32 [16384], P(('row', 'col')), may hold values from 0 to 127
- p_pattern: int32 [128, 128], P('row', 'col'), may hold values from 0 to 1, as said below
- c_pattern: int32 [128, 128], P('row', 'col'), may hold values from 0 to 1, as said below
- occupations: float32 [8192], P('row'), may hold values from 0.1 to 0.9
Outputs:
- purified: float32 [8192, 8192], P(('row', 'layer'), 'col')
Inputs may be any that keep to these rules, and one draw needn't show every extreme that they name: `task_owner`: the 128 tasks of one index of row and col name each owner at most 2 times. `task_slot`: a block of the owner's 8 x 16 blocks, row-major. `p_pattern`: 0 or 1; every diagonal block is 1. `c_pattern`: 0 or 1; every diagonal block is 1.
All inputs are finite; a program needn't handle non-finite values.
Results may differ from a plain program's by a relative error of at most 0.025.
Values may be sent and summed in bfloat16 or wider, within the bound.
A program may use at most 64 MiB of HBM per device.

v0:
```python
import jax
import jax.numpy as jnp
from jax import lax
from jax.sharding import PartitionSpec as P

BLK = 64


def expand_blocks(pattern):
    return jnp.repeat(jnp.repeat(pattern.astype(jnp.float32), BLK, axis=0), BLK, axis=1)


def column_units(tile, layers, layer):
    rows, cols = tile.shape
    unit = rows // layers
    split = tile.reshape(rows, cols // (layers * unit), layers, unit)
    picked = lax.dynamic_index_in_dim(split, layer, axis=2, keepdims=False)
    return picked.reshape(rows, cols // layers)


def row_unit(tile, layers, layer):
    unit = tile.shape[0] // layers
    return lax.dynamic_slice_in_dim(tile, layer * unit, unit, 0)


def fold_rows(piece_rows, left_panel):
    return jnp.dot(
        left_panel,
        lax.all_gather(piece_rows, "row", axis=0, tiled=True),
        preferred_element_type=jnp.float32,
    )


def on_device(tasks, task_owner, task_slot, p_pattern, c_pattern, occupations):
    owners = lax.axis_size("row") * lax.axis_size("col")
    task_count = tasks.shape[0]
    capacity = max(2, 2 * task_count // owners)
    block_rows, block_cols = p_pattern.shape
    slots_here = block_rows * block_cols
    owner = task_owner[:, 0]
    same = (owner[:, None] == jnp.arange(owners, dtype=jnp.int32)[None, :]).astype(jnp.int32)
    placed = jnp.sum(jnp.cumsum(same, axis=0) * same, axis=1) - 1
    target = owner * capacity + placed
    send_blocks = jnp.zeros((owners * capacity, BLK * BLK), jnp.bfloat16).at[target].set(tasks)
    send_slots = (
        jnp.full((owners * capacity,), -1.0, jnp.bfloat16)
        .at[target]
        .set(task_slot.astype(jnp.bfloat16))
    )
    got_blocks, got_slots = (
        lax.all_to_all(
            send_blocks.reshape(owners, capacity, BLK * BLK),
            ("row", "col"),
            split_axis=0,
            concat_axis=0,
            tiled=True,
        ),
        lax.all_to_all(
            send_slots.reshape(owners, capacity),
            ("row", "col"),
            split_axis=0,
            concat_axis=0,
            tiled=True,
        ),
    )
    marks = (
        got_slots.reshape(-1).astype(jnp.float32)[:, None]
        == jnp.arange(slots_here, dtype=jnp.float32)[None, :]
    ).astype(jnp.bfloat16)
    summed = lax.dot_general(
        marks,
        got_blocks.reshape(-1, BLK * BLK),
        (((0,), (0,)), ((), ())),
        preferred_element_type=jnp.float32,
    )
    tile_rows = block_rows * BLK
    tile_cols = block_cols * BLK
    assembled = (
        summed.reshape(block_rows, block_cols, BLK, BLK)
        .transpose(0, 2, 1, 3)
        .reshape(tile_rows, tile_cols)
    )
    row_start = lax.axis_index("row") * tile_rows
    col_start = lax.axis_index("col") * tile_cols
    on_diagonal = (row_start + jnp.arange(tile_rows))[:, None] == (
        col_start + jnp.arange(tile_cols)
    )[None, :]
    density = (
        expand_blocks(p_pattern) * assembled + jnp.where(on_diagonal, occupations[:, None], 0.0)
    ).astype(jnp.bfloat16)
    layers = lax.axis_size("layer")
    layer = lax.axis_index("layer")
    left_piece = column_units(density, layers, layer)
    right_piece = row_unit(density, layers, layer)
    left_panel = lax.all_gather(left_piece, "col", axis=1, tiled=True)
    partial_square = fold_rows(right_piece, left_panel)
    square = lax.psum(partial_square.astype(jnp.bfloat16), "layer").astype(jnp.float32)
    square_rows = row_unit(square, layers, layer)
    partial_cube = fold_rows(square_rows.astype(jnp.bfloat16), left_panel)
    cube_rows = row_unit(
        lax.psum(partial_cube.astype(jnp.bfloat16), "layer").astype(jnp.float32), layers, layer
    )
    mask_rows = row_unit(expand_blocks(c_pattern), layers, layer)
    return mask_rows * (3.0 * square_rows - 2.0 * cube_rows)


def solution(mesh):
    return jax.shard_map(
        on_device,
        mesh=mesh,
        in_specs=(
            P(("row", "col"), None),
            P(("row", "col"), None),
            P(("row", "col")),
            P("row", "col"),
            P("row", "col"),
            P("row"),
        ),
        out_specs=P(("row", "layer"), "col"),
        check_vma=False,
    )
```

profile of v0, /device:TPU:1, one launch (start us, length us, event | category | flops | bytes accessed | tf_op | source)
XLA Modules:
  0.0 508.8 jit_solution(2555189373644705348)
XLA Ops:
  6.5 0.7 convert_element_type.47
  7.2 0.7 fusion.12
  7.9 0.2 reduce_window_sum.11
  8.1 0.8 select_reduce_fusion
  8.9 0.7 fusion.13
  9.6 1.3 scatter_custom_fusion
  11.0 0.8 all_to_all.12
  11.8 13.8 %all-to-all-start = ((bf16[128,1,2]{2,1,0:T(2,128)(2,1)}), bf16[128,1,2]{2,1,0:T(2,128)(2,1)S(1)}, u32[]{:S(2)}, u32[]{:S(2)}) async-start(bf16[128,1,2]{2,1,0:T(2,128)(2,1)} %all_to_all.12), calls=%async_computation | async-start | bytes 131072 | tf_op jit(solution)/shard_map/all_to_all | solution.py:58
  25.6 3.4 scatter_custom_fusion.1
  29.0 2.6 reshape.102
  31.6 3.6 all-to-all-done
  35.3 8.2 %all-to-all-start.1 = ((bf16[128,2,4096]{2,1,0:T(2,128)(2,1)}), bf16[128,2,4096]{2,1,0:T(2,128)(2,1)S(1)}, u32[]{:S(2)}, u32[]{:S(2)}) async-start(bf16[128,2,4096]{2,1,0:T(2,128)(2,1)} %reshape.102), calls=%async_computation.1 | async-start | bytes 4194304 | tf_op jit(solution)/shard_map/all_to_all | solution.py:51
  43.5 0.2 all-gather.4.cloned.1.call-start
  43.8 0.1 copy.15
  43.8 0.1 broadcast_in_dim.44
  43.9 0.1 reshape.100
  44.0 0.2 convert_reduce_fusion
  44.2 0.1 reshape.108
  44.4 51.1 %all-to-all-done.1 = bf16[128,2,4096]{2,1,0:T(2,128)(2,1)S(1)} async-done(((bf16[128,2,4096]{2,1,0:T(2,128)(2,1)}), bf16[128,2,4096]{2,1,0:T(2,128)(2,1)S(1)}, u32[]{:S(2)}, u32[]{:S(2)}) %all-to-all-start.1) | async-done | bytes 2097184 | tf_op jit(solution)/shard_map/all_to_all | solution.py:51
  95.5 2.2 reshape.103
  97.7 3.3 copy.17
  101.0 3.2 convolution_bitcast_fusion
  104.2 4.1 reshape.104
  108.3 1.9 constant_dynamic-slice_fusion.2
  110.2 2.4 copy.22
  112.5 0.2 broadcast_in_dim.45
  112.8 1.0 fusion.5
  113.9 0.1 dynamic-slice.2
  114.0 0.1 dynamic-slice.1
  114.0 4.9 reshape.107
  118.9 2.3 constant_dynamic-slice_fusion.1
  121.2 1.6 copy.23
  122.8 1.0 fusion.3
  123.9 38.4 %all-gather.4.cloned.1.call-done = bf16[512,4096]{0,1:T(8,128)(2,1)} async-done(((bf16[512,512]{0,1:T(8,128)(2,1)}), bf16[512,4096]{0,1:T(8,128)(2,1)}) %all-gather.4.cloned.1.call-update) | async-done | bytes 4194320 | tf_op jit(solution)/shard_map/all_gather | solution.py:95
  162.3 85.9 %all-gather.6.cloned.1.call-done = bf16[4096,1024]{0,1:T(8,128)(2,1)} async-done(((bf16[256,1024]{0,1:T(8,128)(2,1)}), bf16[4096,1024]{0,1:T(8,128)(2,1)}) %all-gather.6.cloned.1.call-update) | async-done | bytes 8388624 | tf_op jit(solution)/shard_map/all_gather | solution.py:29
  248.2 10.2 %convolution_convert_fusion.1 = bf16[512,1024]{1,0:T(8,128)(2,1)} fusion(bf16[512,4096]{0,1:T(8,128)(2,1)} %all-gather.4.cloned.1.call-done, bf16[4096,1024]{0,1:T(8,128)(2,1)} %all-gather.6.cloned.1.call-done), kind=kOutput, calls=%fused_computation.4 | convolution fusion | flops 4295491584 | bytes 13631488 | tf_op jit(solution)/shard_map/dot_general | solution.py:27
  258.5 78.6 %all-reduce.3.cloned.1.call-done = bf16[512,1024]{1,0:T(8,128)(2,1)} async-done(((bf16[512,1024]{1,0:T(8,128)(2,1)}), bf16[512,1024]{1,0:T(8,128)(2,1)}) %all-reduce.3.cloned.1.call-update) | async-done | bytes 1048592 | tf_op jit(solution)/shard_map/psum | solution.py:97
  337.1 1.9 convert_convert_fusion
  339.0 0.3 all-reduce.5.cloned.1.call-start
  339.3 72.5 %all-gather.8.cloned.1.call-done = bf16[4096,1024]{1,0:T(8,128)(2,1)} async-done(((bf16[256,1024]{1,0:T(8,128)(2,1)}), bf16[4096,1024]{1,0:T(8,128)(2,1)}) %all-gather.8.cloned.1.call-update) | async-done | bytes 8388624 | tf_op jit(solution)/shard_map/all_gather | solution.py:29
  411.8 10.1 %convolution_convert_fusion = bf16[512,1024]{1,0:T(8,128)(2,1)} fusion(bf16[512,4096]{0,1:T(8,128)(2,1)} %all-gather.4.cloned.1.call-done, bf16[4096,1024]{1,0:T(8,128)(2,1)} %all-gather.8.cloned.1.call-done), kind=kOutput, calls=%fused_computation.3 | convolution fusion | flops 4295491584 | bytes 13631488 | tf_op jit(solution)/shard_map/dot_general | solution.py:27
  422.0 0.1 broadcast_in_dim.42
  422.1 0.1 reshape.98
  422.2 0.3 broadcast_in_dim.43
  422.5 0.1 constant_dynamic-slice_fusion.3
  422.6 0.3 copy.21
  422.9 77.1 %all-reduce.5.cloned.1.call-done = bf16[512,1024]{1,0:T(8,128)(2,1)} async-done(((bf16[512,1024]{1,0:T(8,128)(2,1)}), bf16[512,1024]{1,0:T(8,128)(2,1)}) %all-reduce.5.cloned.1.call-update) | async-done | bytes 1048592 | tf_op jit(solution)/shard_map/psum | solution.py:101
  500.0 2.2 fusion.1
  (24 shorter events, 0.3 us)
Async XLA Ops:
  11.8 23.5 %all-to-all-start = ((bf16[128,1,2]{2,1,0:T(2,128)(2,1)}), bf16[128,1,2]{2,1,0:T(2,128)(2,1)S(1)}, u32[]{:S(2)}, u32[]{:S(2)}) async-start(bf16[128,1,2]{2,1,0:T(2,128)(2,1)} %all_to_all.12), calls=%async_computation | async-start | bytes 131072 | tf_op jit(solution)/shard_map/all_to_all | solution.py:58
  31.6 12.1 %copy-start.2 = (s32[8,16]{1,0:T(8,128)S(1)}, s32[8,16]{1,0:T(8,128)}, u32[]{:S(2)}) copy-start(s32[8,16]{1,0:T(8,128)} %param.9) | copy-start | bytes 1540
  35.3 60.2 %all-to-all-start.1 = ((bf16[128,2,4096]{2,1,0:T(2,128)(2,1)}), bf16[128,2,4096]{2,1,0:T(2,128)(2,1)S(1)}, u32[]{:S(2)}, u32[]{:S(2)}) async-start(bf16[128,2,4096]{2,1,0:T(2,128)(2,1)} %reshape.102), calls=%async_computation.1 | async-start | bytes 4194304 | tf_op jit(solution)/shard_map/all_to_all | solution.py:51
  43.5 118.8 %all-gather.4.cloned.1.call-start = ((), (), s32[]{:S(2)}) async-start(), calls=%async_computation.2 | async-start | bytes 4718592 | tf_op jit(solution)/shard_map/all_gather | solution.py:95
  110.2 2.6 copy-start.1
  113.8 134.4 %all-gather.6.cloned.1.call-start = ((), (), s32[]{:S(2)}) async-start(), calls=%async_computation.3 | async-start | bytes 8912896 | tf_op jit(solution)/shard_map/all_gather | solution.py:29
  123.8 213.3 %all-reduce.3.cloned.1.call-start = ((), (), s32[]{:S(2)}) async-start(), calls=%async_computation.4 | async-start | bytes 2097152 | tf_op jit(solution)/shard_map/psum | solution.py:97
  258.4 153.4 %all-gather.8.cloned.1.call-start = ((), (), s32[]{:S(2)}) async-start(), calls=%async_computation.5 | async-start | bytes 8912896 | tf_op jit(solution)/shard_map/all_gather | solution.py:29
  339.0 82.9 %copy-start.3 = (s32[8,16]{1,0:T(8,128)S(1)}, s32[8,16]{1,0:T(8,128)}, u32[]{:S(2)}) copy-start(s32[8,16]{1,0:T(8,128)} %param.10) | copy-start | bytes 1540
  339.0 161.0 %all-reduce.5.cloned.1.call-start = ((), (), s32[]{:S(2)}) async-start(), calls=%async_computation.6 | async-start | bytes 2097152 | tf_op jit(solution)/shard_map/psum | solution.py:101
  422.5 77.6 %copy-start = (bf16[512,1024]{1,0:T(8,128)(2,1)S(1)}, bf16[512,1024]{1,0:T(8,128)(2,1)}, u32[]{:S(2)}) copy-start(bf16[512,1024]{1,0:T(8,128)(2,1)} %all-reduce.3.cloned.1.call-done) | copy-start | bytes 3145732
Sparse Core Ops, SparseCore 0:
  114.0 48.3 all-gather.3
  164.7 83.4 all-gather.5
  258.5 78.5 all-reduce.2
  339.7 72.0 all-gather.7
  422.1 77.9 all-reduce.4
where the time goes:
time: 510 us; the launch traced here: 509 us
  waiting for transfers between devices  407 us (80%)
  local copies, waits for them, and re-layouts  32.5 us (6%)
  matrix products  23.5 us (5%)
  starting transfers between devices  22.7 us (4%)
  between operations  13.4 us (3%)
  other arithmetic  9.42 us (2%)
    all_gather x2, waiting for transfers between devices, fold_rows(): lax.all_gather(piece_rows, 'row', axis=0, tiled=True)  158 us
    psum x1, waiting for transfers between devices, on_device(): lax.psum(partial_square.astype(jnp.bfloat16), 'layer').astype(jnp.float32)  78.6 us
    psum x1, waiting for transfers between devices, on_device(): lax.psum(partial_cube.astype(jnp.bfloat16), 'layer').astype(jnp.float32)  77.1 us
    all_to_all x1, waiting for transfers between devices, on_device(): lax.all_to_all(send_blocks.reshape(owners, capacity, BLK * BLK), ('row',...  51.1 us
    all_gather x1, waiting for transfers between devices, on_device(): left_panel = lax.all_gather(left_piece, 'col', axis=1, tiled=True)  38.4 us
    dot_general x2, matrix products, fold_rows(): jnp.dot(left_panel, lax.all_gather(piece_rows, 'row', axis=0, tiled=True)...  20.3 us
    all_to_all x1, starting transfers between devices, on_device(): lax.all_to_all(send_slots.reshape(owners, capacity), ('row', 'col'), spli...  13.8 us
  transfers between devices with their start and end apart: 7, of which 7 were waited for; matrix products, arithmetic and copies ran while one was open for 3% of the time, Pallas kernels for 0%

commit v1 on v0

--- a/solution.py
+++ b/solution.py
@@ -4,6 +4,7 @@
 from jax.sharding import PartitionSpec as P
 
 BLK = 64
+levels_all_recover = lambda chunk: jnp.sum(lax.all_gather(chunk, "layer"), 0)
 
 
 def expand_blocks(pattern):
@@ -98,7 +99,7 @@
     square_rows = row_unit(square, layers, layer)
     partial_cube = fold_rows(square_rows.astype(jnp.bfloat16), left_panel)
     cube_rows = row_unit(
-        lax.psum(partial_cube.astype(jnp.bfloat16), "layer").astype(jnp.float32), layers, layer
+        levels_all_recover(partial_cube.astype(jnp.bfloat16)).astype(jnp.float32), layers, layer
     )
     mask_rows = row_unit(expand_blocks(c_pattern), layers, layer)
     return mask_rows * (3.0 * square_rows - 2.0 * cube_rows)

time: 510 us -> 498 us (0.976)
  waiting for transfers between devices: 407 us -> 394 us
    psum x1 -> x0, waiting for transfers between devices: 77.1 us -> none  [on_device(): lax.psum(partial_cube.astype(jnp.bfloat16), 'layer').astype(jnp.float32)]
    all_gather x0 -> x1, waiting for transfers between devices: none -> 64.1 us  [lax.all_gather(chunk, 'layer')]
  transfers between devices with their start and end apart: 7 -> 7, of which waited for: 7 -> 7; matrix products, arithmetic and copies ran while one was open for 3% -> 4% of each run, Pallas kernels for 0% -> 0%
where the time goes in v1:
time: 498 us; the launch traced here: 497 us
  waiting for transfers between devices  394 us (79%)
  local copies, waits for them, and re-layouts  32.5 us (7%)
  matrix products  23.5 us (5%)
  starting transfers between devices  22.7 us (5%)
  between operations  13.4 us (3%)
  other arithmetic  10.5 us (2%)
    all_gather x2, waiting for transfers between devices, fold_rows(): lax.all_gather(piece_rows, 'row', axis=0, tiled=True)  158 us
    psum x1, waiting for transfers between devices, on_device(): lax.psum(partial_square.astype(jnp.bfloat16), 'layer').astype(jnp.float32)  78.6 us
    all_gather x1, waiting for transfers between devices, lax.all_gather(chunk, 'layer')  64.1 us
    all_to_all x1, waiting for transfers between devices, on_device(): lax.all_to_all(send_blocks.reshape(owners, capacity, BLK * BLK), ('row',...  51.1 us
    all_gather x1, waiting for transfers between devices, on_device(): left_panel = lax.all_gather(left_piece, 'col', axis=1, tiled=True)  38.4 us
    dot_general x2, matrix products, fold_rows(): jnp.dot(left_panel, lax.all_gather(piece_rows, 'row', axis=0, tiled=True)...  20.3 us
    all_to_all x1, starting transfers between devices, on_device(): lax.all_to_all(send_slots.reshape(owners, capacity), ('row', 'col'), spli...  13.8 us
  transfers between devices with their start and end apart: 7, of which 7 were waited for; matrix products, arithmetic and copies ran while one was open for 4% of the time, Pallas kernels for 0%

profile of v1, /device:TPU:1, one launch (start us, length us, event | category | flops | bytes accessed | tf_op | source)
XLA Modules:
  0.0 496.9 jit_solution(7564973283632156204)
XLA Ops:
  6.5 0.7 convert_element_type.49
  7.2 0.7 fusion.12
  7.9 0.2 reduce_window_sum.11
  8.1 0.8 select_reduce_fusion
  8.9 0.7 fusion.13
  9.6 1.3 scatter_custom_fusion
  11.0 0.8 all_to_all.12
  11.8 13.8 %all-to-all-start = ((bf16[128,1,2]{2,1,0:T(2,128)(2,1)}), bf16[128,1,2]{2,1,0:T(2,128)(2,1)S(1)}, u32[]{:S(2)}, u32[]{:S(2)}) async-start(bf16[128,1,2]{2,1,0:T(2,128)(2,1)} %all_to_all.12), calls=%async_computation | async-start | bytes 131072 | tf_op jit(solution)/shard_map/all_to_all | solution.py:59
  25.6 3.4 scatter_custom_fusion.1
  29.0 2.6 reshape.102
  31.6 3.6 all-to-all-done
  35.3 8.2 %all-to-all-start.1 = ((bf16[128,2,4096]{2,1,0:T(2,128)(2,1)}), bf16[128,2,4096]{2,1,0:T(2,128)(2,1)S(1)}, u32[]{:S(2)}, u32[]{:S(2)}) async-start(bf16[128,2,4096]{2,1,0:T(2,128)(2,1)} %reshape.102), calls=%async_computation.1 | async-start | bytes 4194304 | tf_op jit(solution)/shard_map/all_to_all | solution.py:52
  43.5 0.2 all-gather.6.cloned.1.call-start
  43.8 0.1 broadcast_in_dim.44
  43.9 0.1 reshape.100
  44.0 0.2 convert_reduce_fusion
  44.2 0.1 reshape.108
  44.4 51.1 %all-to-all-done.1 = bf16[128,2,4096]{2,1,0:T(2,128)(2,1)S(1)} async-done(((bf16[128,2,4096]{2,1,0:T(2,128)(2,1)}), bf16[128,2,4096]{2,1,0:T(2,128)(2,1)S(1)}, u32[]{:S(2)}, u32[]{:S(2)}) %all-to-all-start.1) | async-done | bytes 2097184 | tf_op jit(solution)/shard_map/all_to_all | solution.py:52
  95.5 2.2 reshape.103
  97.7 3.3 copy.17
  101.0 3.2 convolution_bitcast_fusion
  104.2 4.1 reshape.104
  108.3 1.9 constant_dynamic-slice_fusion.2
  110.2 2.4 copy.22
  112.5 0.2 broadcast_in_dim.45
  112.8 1.0 fusion.5
  113.9 0.1 dynamic-slice.2
  114.0 0.1 dynamic-slice.1
  114.0 4.9 reshape.107
  118.9 2.3 constant_dynamic-slice_fusion.1
  121.2 1.6 copy.23
  122.8 1.0 fusion.3
  123.9 38.4 %all-gather.6.cloned.1.call-done = bf16[512,4096]{0,1:T(8,128)(2,1)} async-done(((bf16[512,512]{0,1:T(8,128)(2,1)}), bf16[512,4096]{0,1:T(8,128)(2,1)}) %all-gather.6.cloned.1.call-update) | async-done | bytes 4194320 | tf_op jit(solution)/shard_map/all_gather | solution.py:96
  162.3 85.9 %all-gather.8.cloned.1.call-done = bf16[4096,1024]{0,1:T(8,128)(2,1)} async-done(((bf16[256,1024]{0,1:T(8,128)(2,1)}), bf16[4096,1024]{0,1:T(8,128)(2,1)}) %all-gather.8.cloned.1.call-update) | async-done | bytes 8388624 | tf_op jit(solution)/shard_map/all_gather | solution.py:30
  248.2 10.2 %convolution_convert_fusion.1 = bf16[512,1024]{1,0:T(8,128)(2,1)} fusion(bf16[512,4096]{0,1:T(8,128)(2,1)} %all-gather.6.cloned.1.call-done, bf16[4096,1024]{0,1:T(8,128)(2,1)} %all-gather.8.cloned.1.call-done), kind=kOutput, calls=%fused_computation.4 | convolution fusion | flops 4295491584 | bytes 13631488 | tf_op jit(solution)/shard_map/dot_general | solution.py:28
  258.5 78.6 %all-reduce.2.cloned.1.call-done = bf16[512,1024]{1,0:T(8,128)(2,1)} async-done(((bf16[512,1024]{1,0:T(8,128)(2,1)}), bf16[512,1024]{1,0:T(8,128)(2,1)}) %all-reduce.2.cloned.1.call-update) | async-done | bytes 1048592 | tf_op jit(solution)/shard_map/psum | solution.py:98
  337.1 1.9 convert_convert_fusion
  339.0 0.3 all-gather.12.cloned.1.call-start
  339.3 72.5 %all-gather.10.cloned.1.call-done = bf16[4096,1024]{1,0:T(8,128)(2,1)} async-done(((bf16[256,1024]{1,0:T(8,128)(2,1)}), bf16[4096,1024]{1,0:T(8,128)(2,1)}) %all-gather.10.cloned.1.call-update) | async-done | bytes 8388624 | tf_op jit(solution)/shard_map/all_gather | solution.py:30
  411.8 10.1 %convolution_convert_fusion = bf16[512,1024]{1,0:T(8,128)(2,1)} fusion(bf16[512,4096]{0,1:T(8,128)(2,1)} %all-gather.6.cloned.1.call-done, bf16[4096,1024]{1,0:T(8,128)(2,1)} %all-gather.10.cloned.1.call-done), kind=kOutput, calls=%fused_computation.3 | convolution fusion | flops 4295491584 | bytes 13631488 | tf_op jit(solution)/shard_map/dot_general | solution.py:28
  422.0 0.1 broadcast_in_dim.42
  422.1 0.1 reshape.98
  422.2 0.3 broadcast_in_dim.43
  422.5 0.1 constant_dynamic-slice_fusion.3
  422.6 0.3 copy.21
  422.9 64.1 %all-gather.12.cloned.1.call-done = bf16[1024,1024]{1,0:T(8,128)(2,1)} async-done(((bf16[512,1024]{1,0:T(8,128)(2,1)}), bf16[1024,1024]{1,0:T(8,128)(2,1)}) %all-gather.12.cloned.1.call-update) | async-done | bytes 2097168 | tf_op jit(solution)/shard_map/all_gather | solution.py:7
  487.0 2.2 reduce_sum.22
  489.2 1.2 fusion.1
  (25 shorter events, 0.4 us)
Async XLA Ops:
  11.8 23.5 %all-to-all-start = ((bf16[128,1,2]{2,1,0:T(2,128)(2,1)}), bf16[128,1,2]{2,1,0:T(2,128)(2,1)S(1)}, u32[]{:S(2)}, u32[]{:S(2)}) async-start(bf16[128,1,2]{2,1,0:T(2,128)(2,1)} %all_to_all.12), calls=%async_computation | async-start | bytes 131072 | tf_op jit(solution)/shard_map/all_to_all | solution.py:59
  31.6 12.1 %copy-start.2 = (s32[8,16]{1,0:T(8,128)S(1)}, s32[8,16]{1,0:T(8,128)}, u32[]{:S(2)}) copy-start(s32[8,16]{1,0:T(8,128)} %param.9) | copy-start | bytes 1540
  35.3 60.2 %all-to-all-start.1 = ((bf16[128,2,4096]{2,1,0:T(2,128)(2,1)}), bf16[128,2,4096]{2,1,0:T(2,128)(2,1)S(1)}, u32[]{:S(2)}, u32[]{:S(2)}) async-start(bf16[128,2,4096]{2,1,0:T(2,128)(2,1)} %reshape.102), calls=%async_computation.1 | async-start | bytes 4194304 | tf_op jit(solution)/shard_map/all_to_all | solution.py:52
  43.5 118.8 %all-gather.6.cloned.1.call-start = ((), (), s32[]{:S(2)}) async-start(), calls=%async_computation.2 | async-start | bytes 4718592 | tf_op jit(solution)/shard_map/all_gather | solution.py:96
  110.2 2.6 copy-start.1
  113.8 134.4 %all-gather.8.cloned.1.call-start = ((), (), s32[]{:S(2)}) async-start(), calls=%async_computation.3 | async-start | bytes 8912896 | tf_op jit(solution)/shard_map/all_gather | solution.py:30
  123.8 213.3 %all-reduce.2.cloned.1.call-start = ((), (), s32[]{:S(2)}) async-start(), calls=%async_computation.4 | async-start | bytes 2097152 | tf_op jit(solution)/shard_map/psum | solution.py:98
  258.4 153.4 %all-gather.10.cloned.1.call-start = ((), (), s32[]{:S(2)}) async-start(), calls=%async_computation.5 | async-start | bytes 8912896 | tf_op jit(solution)/shard_map/all_gather | solution.py:30
  339.0 82.9 %copy-start.3 = (s32[8,16]{1,0:T(8,128)S(1)}, s32[8,16]{1,0:T(8,128)}, u32[]{:S(2)}) copy-start(s32[8,16]{1,0:T(8,128)} %param.10) | copy-start | bytes 1540
  339.0 148.0 %all-gather.12.cloned.1.call-start = ((), (), s32[]{:S(2)}) async-start(), calls=%async_computation.6 | async-start | bytes 3145728 | tf_op jit(solution)/shard_map/all_gather | solution.py:7
  422.9 66.2 %copy-start = (bf16[512,1024]{1,0:T(8,128)(2,1)S(1)}, bf16[512,1024]{1,0:T(8,128)(2,1)}, u32[]{:S(2)}) copy-start(bf16[512,1024]{1,0:T(8,128)(2,1)} %all-reduce.2.cloned.1.call-done) | copy-start | bytes 3145732
Sparse Core Ops, SparseCore 0:
  114.0 48.3 all-gather.5
  164.7 83.4 all-gather.7
  258.5 78.5 all-reduce.1
  339.7 72.0 all-gather.9
  422.1 64.8 all-gather.11
